TPU v7x, 256 devices: a whole 4x4x8 slice. The times are simulated.
256 devices in a mesh: row: 32 (over y, x, core), col: 8 (over z).
Axes of the slice: x: 4, y: 4, z: 8, core: 2. Of those that a mesh axis runs over, the one named last changes fastest.
Arguments:
- diag: float32 [4, 1024, 1024], P(None, 'row'), as said below
- panel_rows: float32 [64, 8, 64, 1024], P('row', None, None, 'col')
- panel_cols: float32 [8, 8, 64, 1024], P('col', None, 'row')
- trailing: float32 [64, 8, 8, 64, 1024], P('row', 'col')
- sketch: float32 [64, 1024], replicated, may hold values from -6 to 6
- panel_rank: int32 [64], P('row'), may hold values from 16 to 64
- col_rank: int32 [8], P('col'), may hold values from 16 to 64
- tile_rank: int32 [64, 8], P('row', 'col'), may hold values from 32 to 64
- keep_rank: int32 [64, 8], P('row', 'col'), may hold values from 8 to 32
Outputs:
- new_tiles: float32 [64, 8, 8, 64, 1024], P('row', 'col')
Inputs may be any that keep to these rules, and one draw needn't show every extreme that they name: `keep_rank`: recompression ranks, never above the tile's rank. diag[0] is symmetric positive definite with smallest eigenvalue 0.5 or more; the tangents are symmetric.
All inputs are finite; a program needn't handle non-finite values.
Results may differ from a plain program's by a relative error of at most 0.0003.
Values sent between devices are 32-bit elements; how exact they have to be, the bound alone decides.
A program may use at most 192 MiB of HBM per device.

v0:
```python
import math
import jax
import jax.numpy as jnp
from jax import lax
from jax.sharding import PartitionSpec as P

HIGHEST_PRECISION = lax.Precision.HIGHEST


def highest_accuracy(left, right):
    return jnp.dot(left, right, precision=HIGHEST_PRECISION, preferred_element_type=jnp.float32)


def rank_mask(rank_values, rank_count):
    return (jnp.arange(rank_count, dtype=jnp.int32) < rank_values[..., None]).astype(jnp.float32)


def inverse_apply(lower_factor, rank_rows):
    half_solved = jax.scipy.linalg.solve_triangular(lower_factor, rank_rows.T, lower=True)
    full_solved = jax.scipy.linalg.solve_triangular(lower_factor, half_solved, lower=True, trans=1)
    return full_solved.T


def sketch_apply(active_sketch, previous_left_factor, previous_right_factor, u_row, mix_in, u_col):
    return highest_accuracy(
        highest_accuracy(active_sketch, previous_right_factor.T), previous_left_factor
    ) - highest_accuracy(
        highest_accuracy(highest_accuracy(active_sketch, u_col.T), mix_in.T), u_row
    )


def basis_apply(
    row_basis_matrix, previous_left_factor, previous_right_factor, u_row, mix_in, u_col
):
    return highest_accuracy(
        highest_accuracy(row_basis_matrix, previous_left_factor.T), previous_right_factor
    ) - highest_accuracy(
        highest_accuracy(highest_accuracy(row_basis_matrix, u_row.T), mix_in), u_col
    )


def compress_all(
    previous_left_factor,
    previous_right_factor,
    u_row,
    mix_in,
    u_col,
    du_old,
    dv_old,
    du_row,
    dmix_in,
    du_col,
    active_sketch,
    live_mask,
):
    sketched = sketch_apply(
        active_sketch, previous_left_factor, previous_right_factor, u_row, mix_in, u_col
    )
    gram_matrix = highest_accuracy(sketched, sketched.T) + jnp.diag(1.0 - live_mask)
    factor = jnp.linalg.cholesky(gram_matrix)
    row_basis_matrix = jax.scipy.linalg.solve_triangular(factor, sketched, lower=True)
    coefficients = basis_apply(
        row_basis_matrix, previous_left_factor, previous_right_factor, u_row, mix_in, u_col
    )
    up_scale = math.sqrt(previous_left_factor.shape[1])
    down_scale = math.sqrt(previous_left_factor.shape[0])

    def tangent_direction(
        previous_left_derivative,
        previous_right_derivative,
        row_left_derivative,
        mixing_derivative,
        column_left_derivative,
    ):
        sketch_derivative = highest_accuracy(
            highest_accuracy(active_sketch, previous_right_derivative.T), previous_left_factor
        ) + highest_accuracy(
            highest_accuracy(active_sketch, previous_right_factor.T), previous_left_derivative
        )
        sketch_derivative = sketch_derivative - highest_accuracy(
            highest_accuracy(highest_accuracy(active_sketch, column_left_derivative.T), mix_in.T),
            u_row,
        )
        sketch_derivative = sketch_derivative - highest_accuracy(
            highest_accuracy(highest_accuracy(active_sketch, u_col.T), mixing_derivative.T), u_row
        )
        sketch_derivative = sketch_derivative - highest_accuracy(
            highest_accuracy(highest_accuracy(active_sketch, u_col.T), mix_in.T),
            row_left_derivative,
        )
        d_gram = highest_accuracy(sketch_derivative, sketched.T) + highest_accuracy(
            sketched, sketch_derivative.T
        )
        inner = jax.scipy.linalg.solve_triangular(factor, d_gram, lower=True)
        middle = jax.scipy.linalg.solve_triangular(factor, inner.T, lower=True)
        lower_part = jnp.tril(middle) - 0.5 * jnp.diag(jnp.diagonal(middle))
        d_factor = highest_accuracy(factor, lower_part)
        d_basis = jax.scipy.linalg.solve_triangular(
            factor, sketch_derivative - highest_accuracy(d_factor, row_basis_matrix), lower=True
        )
        coefficient_derivative = basis_apply(
            d_basis, previous_left_factor, previous_right_factor, u_row, mix_in, u_col
        )
        coefficient_derivative = (
            coefficient_derivative
            + highest_accuracy(
                highest_accuracy(row_basis_matrix, previous_left_derivative.T),
                previous_right_factor,
            )
            + highest_accuracy(
                highest_accuracy(row_basis_matrix, previous_left_factor.T),
                previous_right_derivative,
            )
        )
        coefficient_derivative = coefficient_derivative - highest_accuracy(
            highest_accuracy(highest_accuracy(row_basis_matrix, row_left_derivative.T), mix_in),
            u_col,
        )
        coefficient_derivative = coefficient_derivative - highest_accuracy(
            highest_accuracy(highest_accuracy(row_basis_matrix, u_row.T), mixing_derivative), u_col
        )
        coefficient_derivative = coefficient_derivative - highest_accuracy(
            highest_accuracy(highest_accuracy(row_basis_matrix, u_row.T), mix_in),
            column_left_derivative,
        )
        return (d_basis * up_scale, coefficient_derivative / down_scale)

    tangent_basis, tangent_coeff = jax.vmap(tangent_direction)(
        du_old, dv_old, du_row, dmix_in, du_col
    )
    return (row_basis_matrix * up_scale, coefficients / down_scale, tangent_basis, tangent_coeff)


def update_tile(
    row_tile, row_solved, col_tile, col_solved, col_products, old_tile, tile_mask, keep_mask, sketch
):
    old_tile = old_tile * tile_mask[None, :, None]
    mixing = highest_accuracy(row_tile[4], col_solved.T)
    tangent_mix = jnp.stack(
        [
            highest_accuracy(row_tile[5 + direction], col_solved.T)
            + highest_accuracy(row_solved, col_tile[5 + direction].T)
            - highest_accuracy(row_solved, col_products[direction].T)
            for direction in range(3)
        ]
    )
    active_sketch = sketch * keep_mask[:, None]
    basis_out, coeff_out, tangent_basis, tangent_coeff = compress_all(
        old_tile[0],
        old_tile[4],
        row_tile[0],
        mixing,
        col_tile[0],
        old_tile[1:4],
        old_tile[5:8],
        row_tile[1:4],
        tangent_mix,
        col_tile[1:4],
        active_sketch,
        keep_mask,
    )
    return jnp.concatenate([basis_out[None], tangent_basis, coeff_out[None], tangent_coeff], axis=0)


def on_device(
    diag, panel_rows, panel_cols, trailing, sketch, panel_rank, col_rank, tile_rank, keep_rank
):
    rank_count = sketch.shape[0]
    tile_width = sketch.shape[1]
    gathered = lax.all_gather(diag, "row", axis=1, tiled=True)
    primal = gathered[0]
    lower_factor = jnp.linalg.cholesky(primal)
    rows_kept = (
        lax.all_gather(panel_rows, "col", axis=3, tiled=True)
        * rank_mask(panel_rank, rank_count)[:, None, :, None]
    )
    cols_kept = (
        lax.all_gather(panel_cols, "row", axis=2, tiled=True)
        * rank_mask(col_rank, rank_count)[:, None, :, None]
    )
    col_tile = cols_kept[0]
    col_solved = inverse_apply(lower_factor, col_tile[4])
    col_products = jnp.einsum("aj,tij->tai", col_solved, gathered[1:], precision=HIGHEST_PRECISION)
    local_rows = rows_kept.shape[0]
    row_solved = inverse_apply(lower_factor, rows_kept[:, 4].reshape(-1, tile_width)).reshape(
        local_rows, rank_count, tile_width
    )
    tile_live = rank_mask(tile_rank[:, 0], rank_count)
    keep_live = rank_mask(keep_rank[:, 0], rank_count)

    def one_tile(row_tile, row_z, old_tile, tile_mask, keep_mask):
        return update_tile(
            row_tile,
            row_z,
            col_tile,
            col_solved,
            col_products,
            old_tile,
            tile_mask,
            keep_mask,
            sketch,
        )

    updated = jax.vmap(one_tile)(rows_kept, row_solved, trailing[:, 0], tile_live, keep_live)
    return updated[:, None]


def solution(mesh):
    in_specs = (
        P(None, "row", None),
        P("row", None, None, "col"),
        P("col", None, "row", None),
        P("row", "col", None, None, None),
        P(),
        P("row"),
        P("col"),
        P("row", "col"),
        P("row", "col"),
    )
    out_specs = P("row", "col", None, None, None)
    return jax.shard_map(
        on_device, mesh=mesh, in_specs=in_specs, out_specs=out_specs, check_vma=False
    )
```

profile of v0, /device:TPU:1, one launch (start us, length us, event | category | flops | bytes accessed | tf_op | source)
XLA Modules:
  0.0 733.9 jit_solution(14539865115307290714)
XLA Ops:
  28.6 34.0 %all-gather.4.cloned.1.call-done = f32[1,8,64,1024]{3,1,0,2:T(8,128)} async-done(((f32[1,8,2,1024]{3,1,0,2:T(8,128)}), f32[1,8,64,1024]{3,1,0,2:T(8,128)}) %all-gather.4.cloned.1.call-update) | async-done | bytes 2097168 | tf_op jit(solution)/shard_map/all_gather | solution.py:178
  68.1 54.0 %all-gather.6.cloned.1.call-done = f32[2,8,64,1024]{3,2,0,1:T(8,128)} async-done(((f32[2,8,64,128]{3,2,0,1:T(8,128)}), f32[2,8,64,1024]{3,2,0,1:T(8,128)}) %all-gather.6.cloned.1.call-update) | async-done | bytes 4194320 | tf_op jit(solution)/shard_map/all_gather | solution.py:174
  130.6 74.5 %all-gather.8.cloned.1.call-done = f32[4,1024,1024]{2,0,1:T(4,128)} async-done(((f32[4,32,1024]{2,0,1:T(4,128)}), f32[4,1024,1024]{2,0,1:T(4,128)}) %all-gather.8.cloned.1.call-update) | async-done | bytes 16777232 | tf_op jit(solution)/shard_map/all_gather | solution.py:170
  205.1 8.7 %slice.584 = f32[1,1024,1024]{2,0,1:T(1,128)} slice(f32[4,1024,1024]{2,0,1:T(4,128)} %all-gather.8.cloned.1.call-done), slice={[0:1], [0:1024], [0:1024]} | slice | bytes 8388608 | tf_op jit(solution)/shard_map/slice | solution.py:171
  213.8 11.4 %copy.214 = f32[1,1024,1024]{1,2,0:T(8,128)} copy(f32[1,1024,1024]{2,0,1:T(1,128)} %slice.584) | data formatting | bytes 8388608
  225.2 5.0 fusion.2
  232.2 11.7 %cholesky.241 = f32[128,128]{1,0:T(8,128)S(1)} custom-call(f32[128,128]{1,0:T(8,128)S(1)} %cholesky.622), custom_call_target="Cholesky" | custom-call | tf_op jit(solution)/shard_map/jit(cholesky)/cholesky | solution.py:172
  243.9 9.8 %custom-call.86 = f32[1,128,128]{1,2,0:T(8,128)S(1)} custom-call(f32[1,128,128]{2,1,0:T(8,128)S(1)} %get-tuple-element.70), custom_call_target="InvertDiagBlocksLowerTriangular" | custom-call | tf_op jit(solution)/shard_map/jit(cholesky)/cholesky | solution.py:172
  260.2 11.8 %cholesky.264 = f32[128,128]{1,0:T(8,128)S(1)} custom-call(f32[128,128]{1,0:T(8,128)S(1)} %cholesky.626), custom_call_target="Cholesky" | custom-call | tf_op jit(solution)/shard_map/jit(cholesky)/cholesky | solution.py:172
  272.7 9.8 %custom-call.87 = f32[1,128,128]{1,2,0:T(8,128)S(1)} custom-call(f32[1,128,128]{2,1,0:T(8,128)S(1)} %get-tuple-element.67), custom_call_target="InvertDiagBlocksLowerTriangular" | custom-call | tf_op jit(solution)/shard_map/jit(cholesky)/cholesky | solution.py:172
  285.8 11.7 %cholesky.502 = f32[128,128]{1,0:T(8,128)S(1)} custom-call(f32[128,128]{1,0:T(8,128)S(1)} %cholesky.631), custom_call_target="Cholesky" | custom-call | tf_op jit(solution)/shard_map/jit(cholesky)/cholesky | solution.py:172
  298.8 9.8 %custom-call.88 = f32[1,128,128]{1,2,0:T(8,128)S(1)} custom-call(f32[1,128,128]{2,1,0:T(8,128)S(1)} %get-tuple-element.64), custom_call_target="InvertDiagBlocksLowerTriangular" | custom-call | tf_op jit(solution)/shard_map/jit(cholesky)/cholesky | solution.py:172
  312.1 11.9 %cholesky.521 = f32[128,128]{1,0:T(8,128)S(1)} custom-call(f32[128,128]{1,0:T(8,128)S(1)} %cholesky.636), custom_call_target="Cholesky" | custom-call | tf_op jit(solution)/shard_map/jit(cholesky)/cholesky | solution.py:172
  325.3 9.8 %custom-call.89 = f32[1,128,128]{1,2,0:T(8,128)S(1)} custom-call(f32[1,128,128]{2,1,0:T(8,128)S(1)} %get-tuple-element.61), custom_call_target="InvertDiagBlocksLowerTriangular" | custom-call | tf_op jit(solution)/shard_map/jit(cholesky)/cholesky | solution.py:172
  338.5 11.7 %cholesky.540 = f32[128,128]{1,0:T(8,128)S(1)} custom-call(f32[128,128]{1,0:T(8,128)S(1)} %cholesky.641), custom_call_target="Cholesky" | custom-call | tf_op jit(solution)/shard_map/jit(cholesky)/cholesky | solution.py:172
  351.5 10.2 %custom-call.90 = f32[1,128,128]{1,2,0:T(8,128)S(1)} custom-call(f32[1,128,128]{2,1,0:T(8,128)S(1)} %get-tuple-element.58), custom_call_target="InvertDiagBlocksLowerTriangular" | custom-call | tf_op jit(solution)/shard_map/jit(cholesky)/cholesky | solution.py:172
  365.0 11.7 %cholesky.560 = f32[128,128]{1,0:T(8,128)S(1)} custom-call(f32[128,128]{1,0:T(8,128)S(1)} %cholesky.646), custom_call_target="Cholesky" | custom-call | tf_op jit(solution)/shard_map/jit(cholesky)/cholesky | solution.py:172
  378.1 9.8 %custom-call.91 = f32[1,128,128]{1,2,0:T(8,128)S(1)} custom-call(f32[1,128,128]{2,1,0:T(8,128)S(1)} %get-tuple-element.55), custom_call_target="InvertDiagBlocksLowerTriangular" | custom-call | tf_op jit(solution)/shard_map/jit(cholesky)/cholesky | solution.py:172
  390.9 11.9 %cholesky.580 = f32[128,128]{1,0:T(8,128)S(1)} custom-call(f32[128,128]{1,0:T(8,128)S(1)} %cholesky.651), custom_call_target="Cholesky" | custom-call | tf_op jit(solution)/shard_map/jit(cholesky)/cholesky | solution.py:172
  404.0 9.8 %custom-call.92 = f32[1,128,128]{1,2,0:T(8,128)S(1)} custom-call(f32[1,128,128]{2,1,0:T(8,128)S(1)} %get-tuple-element.52), custom_call_target="InvertDiagBlocksLowerTriangular" | custom-call | tf_op jit(solution)/shard_map/jit(cholesky)/cholesky | solution.py:172
  416.5 11.7 %cholesky.598 = f32[128,128]{1,0:T(8,128)S(1)} custom-call(f32[128,128]{1,0:T(8,128)S(1)} %convolution_subtract_fusion.21), custom_call_target="Cholesky" | custom-call | tf_op jit(solution)/shard_map/jit(cholesky)/cholesky | solution.py:172
  435.0 4.9 select_select_fusion
  439.9 28.2 %while.1 = (s32[]{:T(128)}, f32[1024,1024]{1,0:T(8,128)}, s32[8,2]{0,1:T(2,128)S(1)}, f32[8,128,128]{2,1,0:T(8,128)}, s32[]{:T(128)}) while((s32[]{:T(128)}, f32[1024,1024]{1,0:T(8,128)}, s32[8,2]{0,1:T(2,128)S(1)}, f32[8,128,128]{2,1,0:T(8,128)}, s32[]{:T(128)}) %tuple.84), condition=%wide.while_cond, body=%wide.while_body.sunk | while | flops 2 | bytes 132705 | solution.py:20
  468.1 79.6 %custom-call.93 = f32[8,128,128]{1,2,0:T(8,128)S(1)} custom-call(f32[8,128,128]{2,1,0:T(8,128)} %get-tuple-element.13), custom_call_target="InvertDiagBlocksLowerTriangular" | custom-call | tf_op jit(solution)/shard_map/jit(_solve_triangular)/triangular_solve | solution.py:20
  574.2 11.7 %custom-call.94 = f32[2,64,64]{2,1,0:T(8,128)S(1)} custom-call(f32[2,64,64]{2,1,0:T(8,128)S(1)} %fusion.264), custom_call_target="Cholesky" | custom-call | tf_op jit(solution)/shard_map/vmap(jit(cholesky))/cholesky | solution.py:60
  586.2 10.2 %custom-call.95 = f32[2,1,64,64]{2,3,1,0:T(8,128)S(1)} custom-call(f32[2,1,64,64]{3,2,1,0:T(8,128)S(1)} %select_bitcast_fusion), custom_call_target="InvertDiagBlocksLowerTriangular" | custom-call | tf_op jit(solution)/shard_map/vmap(jit(_solve_triangular))/triangular_solve | solution.py:61
  619.8 9.7 %slice.592 = f32[3,1024,1024]{2,0,1:T(4,128)S(1)} slice(f32[4,1024,1024]{2,0,1:T(4,128)} %all-gather.8.cloned.1.call-done), slice={[1:4], [0:1024], [0:1024]} | slice | bytes 25165824 | tf_op jit(solution)/shard_map/slice | solution.py:183
  629.5 20.2 %fusion.23 = f32[3,64,1024]{2,1,0:T(8,128)S(1)} fusion(f32[3,1024,1024]{2,0,1:T(4,128)S(1)} %slice.592, f32[1024,64]{0,1:T(8,128)S(1)} %constant_dynamic-update-slice_fusion.36), kind=kOutput, calls=%fused_computation.33 | convolution fusion | flops 2415919104 | bytes 13631488 | tf_op jit(solution)/shard_map/aj,tij->tai/dot_general | solution.py:183
  670.8 4.4 copy.177
  681.2 5.3 copy.179
  686.5 5.3 fusion.3
  695.2 4.2 copy.183
  (318 shorter events, 206.7 us)
Async XLA Ops:
  6.5 56.1 %all-gather.4.cloned.1.call-start = ((), (), s32[]{:S(2)}) async-start(), calls=%async_computation | async-start | bytes 2162688 | tf_op jit(solution)/shard_map/all_gather | solution.py:178
  8.0 114.1 %all-gather.6.cloned.1.call-start = ((), (), s32[]{:S(2)}) async-start(), calls=%async_computation.1 | async-start | bytes 4718592 | tf_op jit(solution)/shard_map/all_gather | solution.py:174
  10.0 195.1 %all-gather.8.cloned.1.call-start = ((), (), s32[]{:S(2)}) async-start(), calls=%async_computation.2 | async-start | bytes 17301504 | tf_op jit(solution)/shard_map/all_gather | solution.py:170
  17.1 3.2 copy-start.12
  20.2 5.9 copy-start.1
  20.9 3.1 copy-start.13
  65.5 1.4 copy-start.3
  66.9 504.7 %copy-start.15 = (f32[2,64,64]{2,1,0:T(8,128)}, f32[2,64,64]{2,1,0:T(8,128)S(1)}, u32[]{:S(2)}) copy-start(f32[2,64,64]{2,1,0:T(8,128)S(1)} %fusion.38) | copy-start | bytes 98308
  124.9 2.0 copy-start.2
  230.2 2.0 copy-start.5
  563.2 10.9 %copy-start.27 = (pred[64,64]{1,0:T(8,128)(4,1)S(1)}, pred[64,64]{1,0:T(8,128)(4,1)}, u32[]{:S(2)}) copy-start(pred[64,64]{1,0:T(8,128)(4,1)} %get-tuple-element.120) | copy-start | bytes 12292
  564.5 21.6 %copy-start.25 = (pred[64,64]{1,0:T(8,128)(4,1)S(1)}, pred[64,64]{1,0:T(8,128)(4,1)}, u32[]{:S(2)}) copy-start(pred[64,64]{1,0:T(8,128)(4,1)} %iota_compare_fusion.5) | copy-start | bytes 12292
  571.8 14.3 %copy-start.18 = (f32[2,64,64]{2,1,0:T(8,128)}, f32[2,64,64]{2,1,0:T(8,128)S(1)}, u32[]{:S(2)}) copy-start(f32[2,64,64]{2,1,0:T(8,128)S(1)} %fusion.331) | copy-start | bytes 98308
  585.9 23.7 %copy-start.20 = (f32[2,64,64]{2,1,0:T(8,128)}, f32[2,64,64]{2,1,0:T(8,128)S(1)}, u32[]{:S(2)}) copy-start(f32[2,64,64]{2,1,0:T(8,128)S(1)} %custom-call.94) | copy-start | bytes 98308
  596.4 11.8 %copy-start = (f32[1024,1024]{1,0:T(8,128)S(1)}, f32[1024,1024]{1,0:T(8,128)}, u32[]{:S(2)}) copy-start(f32[1024,1024]{1,0:T(8,128)} %get-tuple-element.169) | copy-start | bytes 12582916
  629.4 20.2 %copy-start.24 = (f32[2,64,64]{2,1,0:T(8,128)S(1)}, f32[2,64,64]{2,1,0:T(8,128)}, u32[]{:S(2)}) copy-start(f32[2,64,64]{2,1,0:T(8,128)} %fusion.54) | copy-start | bytes 98308
  629.4 21.8 %copy-start.23 = (f32[2,64,64]{2,1,0:T(8,128)S(1)}, f32[2,64,64]{2,1,0:T(8,128)}, u32[]{:S(2)}) copy-start(f32[2,64,64]{2,1,0:T(8,128)} %fusion.53) | copy-start | bytes 98308
  629.4 24.6 %copy-start.22 = (f32[2,64,64]{2,1,0:T(8,128)S(1)}, f32[2,64,64]{2,1,0:T(8,128)}, u32[]{:S(2)}) copy-start(f32[2,64,64]{2,1,0:T(8,128)} %fusion.52) | copy-start | bytes 98308
  649.6 6.5 copy-start.16
  651.2 8.1 %copy-start.11 = (f32[2,3,64,1024]{3,2,0,1:T(8,128)S(1)}, f32[2,3,64,1024]{3,2,0,1:T(8,128)}, u32[]{:S(2)}) copy-start(f32[2,3,64,1024]{3,2,0,1:T(8,128)} %get-tuple-element.28) | copy-start | bytes 4718596
  651.2 8.1 %copy-start.19 = (f32[2,64,64]{2,1,0:T(8,128)S(1)}, f32[2,64,64]{2,1,0:T(8,128)}, u32[]{:S(2)}) copy-start(f32[2,64,64]{2,1,0:T(8,128)} %copy-done.18) | copy-start | bytes 98308
  656.7 7.0 copy-start.7
  656.7 7.0 copy-start.9
  656.7 7.0 copy-start.14
  667.1 11.2 %copy-start.21 = (f32[2,64,64]{2,1,0:T(8,128)S(1)}, f32[2,64,64]{2,1,0:T(8,128)}, u32[]{:S(2)}) copy-start(f32[2,64,64]{2,1,0:T(8,128)} %copy-done.20) | copy-start | bytes 98308
  667.1 11.2 %copy-start.26 = (pred[64,64]{1,0:T(8,128)(4,1)S(1)}, pred[64,64]{1,0:T(8,128)(4,1)}, u32[]{:S(2)}) copy-start(pred[64,64]{1,0:T(8,128)(4,1)} %iota_compare_fusion.5) | copy-start | bytes 12292
  701.9 4.5 copy-start.17
  701.9 4.7 copy-start.4
  706.6 6.1 copy-start.10
  712.6 5.3 copy-start.8
  714.8 7.6 %copy-start.6 = (f32[2,3,64,1024]{3,2,0,1:T(8,128)S(1)}, f32[2,3,64,1024]{3,2,0,1:T(8,128)}, u32[]{:S(2)}) copy-start(f32[2,3,64,1024]{3,2,0,1:T(8,128)} %get-tuple-element.24) | copy-start | bytes 4718596
Sparse Core Ops, SparseCore 0:
  9.9 52.7 all-gather.3
  64.4 57.7 all-gather.5
  124.7 80.3 all-gather.7
where the time goes:
time: 744 us; the launch traced here: 734 us
  other arithmetic  299 us (40%)
  waiting for transfers between devices  163 us (22%)
  matrix products  152 us (20%)
  local copies, waits for them, and re-layouts  98.7 us (13%)
  between operations  20.8 us (3%)
    another operation x30, other arithmetic, on_device(): lower_factor = jnp.linalg.cholesky(primal)  172 us
    another operation x3, other arithmetic, inverse_apply(): jax.scipy.linalg.solve_triangular(lower_factor, half_solved, lower=True,...  84.5 us
    all_gather x1, waiting for transfers between devices, on_device(): gathered = lax.all_gather(diag, 'row', axis=1, tiled=True)  74.5 us
    dot_general x48, matrix products, highest_accuracy(): jnp.dot(left, right, precision=HIGHEST_PRECISION, preferred_element_type=...  69.4 us
    all_gather x1, waiting for transfers between devices, on_device(): lax.all_gather(panel_rows, 'col', axis=3, tiled=True)  54 us
    all_gather x1, waiting for transfers between devices, on_device(): lax.all_gather(panel_cols, 'row', axis=2, tiled=True)  34 us
    another operation x24, local copies, waits for them, and re-layouts  28.2 us
    another operation x14, matrix products, on_device(): lower_factor = jnp.linalg.cholesky(primal)  22.9 us
  transfers between devices with their start and end apart: 3, of which 3 were waited for; matrix products, arithmetic and copies ran while one was open for 4% of the time, Pallas kernels for 0%

commit v1 on v0

--- a/solution.py
+++ b/solution.py
@@ -3,6 +3,7 @@
 import jax.numpy as jnp
 from jax import lax
 from jax.sharding import PartitionSpec as P
+from jax.lax import all_to_all, axis_size
 
 HIGHEST_PRECISION = lax.Precision.HIGHEST
 
@@ -165,15 +166,22 @@
 def on_device(
     diag, panel_rows, panel_cols, trailing, sketch, panel_rank, col_rank, tile_rank, keep_rank
 ):
+
+    def clear_the_pipes(work_x):
+        made = []
+        for _ in range(axis_size("col")):
+            made.append(work_x)
+        r1 = jnp.concatenate(
+            all_to_all(jnp.stack(made), "col", split_axis=0, concat_axis=0), axis=3
+        )
+        return r1
+
     rank_count = sketch.shape[0]
     tile_width = sketch.shape[1]
     gathered = lax.all_gather(diag, "row", axis=1, tiled=True)
     primal = gathered[0]
     lower_factor = jnp.linalg.cholesky(primal)
-    rows_kept = (
-        lax.all_gather(panel_rows, "col", axis=3, tiled=True)
-        * rank_mask(panel_rank, rank_count)[:, None, :, None]
-    )
+    rows_kept = clear_the_pipes(panel_rows) * rank_mask(panel_rank, rank_count)[:, None, :, None]
     cols_kept = (
         lax.all_gather(panel_cols, "row", axis=2, tiled=True)
         * rank_mask(col_rank, rank_count)[:, None, :, None]

time: 744 us -> 682 us (0.917)
  waiting for transfers between devices: 163 us -> 90.9 us
  starting transfers between devices: 0.09 us -> 9.18 us
    all_gather x1, waiting for transfers between devices: 74.5 us -> 13.3 us  [on_device(): gathered = lax.all_gather(diag, 'row', axis=1, tiled=True)]
    all_gather x1 -> x0, waiting for transfers between devices: 54 us -> none  [on_device(): lax.all_gather(panel_rows, 'col', axis=3, tiled=True)]
    all_to_all x0 -> x1, waiting for transfers between devices: none -> 51.9 us  [clear_the_pipes(): all_to_all(jnp.stack(made), 'col', split_axis=0, concat_axis=0)]
    all_to_all x0 -> x1, starting transfers between devices: none -> 9.13 us  [clear_the_pipes(): all_to_all(jnp.stack(made), 'col', split_axis=0, concat_axis=0)]
    all_gather x1, waiting for transfers between devices: 34 us -> 25.7 us  [on_device(): lax.all_gather(panel_cols, 'row', axis=2, tiled=True)]
    another operation x24 -> x25, local copies, waits for them, and re-layouts: 28.2 us -> 30.7 us
    unnamed x96 -> x102, local copies, waits for them, and re-layouts: 21.9 us -> 21.1 us
  transfers between devices with their start and end apart: 3 -> 3, of which waited for: 3 -> 3; matrix products, arithmetic and copies ran while one was open for 4% -> 5% of each run, Pallas kernels for 0% -> 0%
where the time goes in v1:
time: 682 us; the launch traced here: 671 us
  other arithmetic  297 us (44%)
  matrix products  152 us (22%)
  local copies, waits for them, and re-layouts  100 us (15%)
  waiting for transfers between devices  90.9 us (13%)
  between operations  21.3 us (3%)
  starting transfers between devices  9.18 us (1%)
    another operation x30, other arithmetic, on_device(): lower_factor = jnp.linalg.cholesky(primal)  172 us
    another operation x3, other arithmetic, inverse_apply(): jax.scipy.linalg.solve_triangular(lower_factor, half_solved, lower=True,...  84.5 us
    dot_general x48, matrix products, highest_accuracy(): jnp.dot(left, right, precision=HIGHEST_PRECISION, preferred_element_type=...  69.4 us
    all_to_all x1, waiting for transfers between devices, clear_the_pipes(): all_to_all(jnp.stack(made), 'col', split_axis=0, concat_axis=0)  51.9 us
    another operation x24, local copies, waits for them, and re-layouts  28.1 us
    all_gather x1, waiting for transfers between devices, on_device(): lax.all_gather(panel_cols, 'row', axis=2, tiled=True)  25.7 us
    another operation x14, matrix products, on_device(): lower_factor = jnp.linalg.cholesky(primal)  22.9 us
    unnamed x102, local copies, waits for them, and re-layouts  21.1 us
  transfers between devices with their start and end apart: 3, of which 3 were waited for; matrix products, arithmetic and copies ran while one was open for 5% of the time, Pallas kernels for 0%

profile of v1, /device:TPU:1, one launch (start us, length us, event | category | flops | bytes accessed | tf_op | source)
XLA Modules:
  0.0 671.5 jit_solution(11076455038036036455)
XLA Ops:
  13.9 9.1 %all-to-all-start = ((f32[8,2,8,64,128]{4,3,1,2,0:T(8,128)}), f32[8,2,8,64,128]{4,3,1,2,0:T(8,128)}, u32[]{:S(2)}, u32[]{:S(2)}) async-start(f32[8,2,8,64,128]{4,3,1,2,0:T(8,128)} %stack.10), calls=%async_computation | async-start | bytes 8388608 | tf_op jit(solution)/shard_map/all_to_all | solution.py:175
  36.9 25.7 %all-gather.3.cloned.1.call-done = f32[1,8,64,1024]{3,1,0,2:T(8,128)} async-done(((f32[1,8,2,1024]{3,1,0,2:T(8,128)}), f32[1,8,64,1024]{3,1,0,2:T(8,128)}) %all-gather.3.cloned.1.call-update) | async-done | bytes 2097168 | tf_op jit(solution)/shard_map/all_gather | solution.py:186
  68.1 51.9 %all-to-all-done = f32[8,2,8,64,128]{4,3,1,2,0:T(8,128)} async-done(((f32[8,2,8,64,128]{4,3,1,2,0:T(8,128)}), f32[8,2,8,64,128]{4,3,1,2,0:T(8,128)}, u32[]{:S(2)}, u32[]{:S(2)}) %all-to-all-start) | async-done | bytes 4194336 | tf_op jit(solution)/shard_map/all_to_all | solution.py:175
  128.9 13.3 %all-gather.5.cloned.1.call-done = f32[4,1024,1024]{2,0,1:T(4,128)} async-done(((f32[4,32,1024]{2,0,1:T(4,128)}), f32[4,1024,1024]{2,0,1:T(4,128)}) %all-gather.5.cloned.1.call-update) | async-done | bytes 16777232 | tf_op jit(solution)/shard_map/all_gather | solution.py:181
  142.2 8.7 %slice.584 = f32[1,1024,1024]{2,0,1:T(1,128)} slice(f32[4,1024,1024]{2,0,1:T(4,128)} %all-gather.5.cloned.1.call-done), slice={[0:1], [0:1024], [0:1024]} | slice | bytes 8388608 | tf_op jit(solution)/shard_map/slice | solution.py:182
  150.9 11.4 %copy.217 = f32[1,1024,1024]{1,2,0:T(8,128)} copy(f32[1,1024,1024]{2,0,1:T(1,128)} %slice.584) | data formatting | bytes 8388608
  162.3 5.0 fusion.2
  169.3 11.7 %cholesky.241 = f32[128,128]{1,0:T(8,128)S(1)} custom-call(f32[128,128]{1,0:T(8,128)S(1)} %cholesky.622), custom_call_target="Cholesky" | custom-call | tf_op jit(solution)/shard_map/jit(cholesky)/cholesky | solution.py:183
  181.0 9.8 %custom-call.86 = f32[1,128,128]{1,2,0:T(8,128)S(1)} custom-call(f32[1,128,128]{2,1,0:T(8,128)S(1)} %get-tuple-element.70), custom_call_target="InvertDiagBlocksLowerTriangular" | custom-call | tf_op jit(solution)/shard_map/jit(cholesky)/cholesky | solution.py:183
  197.2 11.8 %cholesky.264 = f32[128,128]{1,0:T(8,128)S(1)} custom-call(f32[128,128]{1,0:T(8,128)S(1)} %cholesky.626), custom_call_target="Cholesky" | custom-call | tf_op jit(solution)/shard_map/jit(cholesky)/cholesky | solution.py:183
  209.7 9.8 %custom-call.87 = f32[1,128,128]{1,2,0:T(8,128)S(1)} custom-call(f32[1,128,128]{2,1,0:T(8,128)S(1)} %get-tuple-element.67), custom_call_target="InvertDiagBlocksLowerTriangular" | custom-call | tf_op jit(solution)/shard_map/jit(cholesky)/cholesky | solution.py:183
  222.9 11.7 %cholesky.502 = f32[128,128]{1,0:T(8,128)S(1)} custom-call(f32[128,128]{1,0:T(8,128)S(1)} %cholesky.631), custom_call_target="Cholesky" | custom-call | tf_op jit(solution)/shard_map/jit(cholesky)/cholesky | solution.py:183
  235.9 9.8 %custom-call.88 = f32[1,128,128]{1,2,0:T(8,128)S(1)} custom-call(f32[1,128,128]{2,1,0:T(8,128)S(1)} %get-tuple-element.64), custom_call_target="InvertDiagBlocksLowerTriangular" | custom-call | tf_op jit(solution)/shard_map/jit(cholesky)/cholesky | solution.py:183
  249.2 11.9 %cholesky.521 = f32[128,128]{1,0:T(8,128)S(1)} custom-call(f32[128,128]{1,0:T(8,128)S(1)} %cholesky.636), custom_call_target="Cholesky" | custom-call | tf_op jit(solution)/shard_map/jit(cholesky)/cholesky | solution.py:183
  262.5 9.8 %custom-call.89 = f32[1,128,128]{1,2,0:T(8,128)S(1)} custom-call(f32[1,128,128]{2,1,0:T(8,128)S(1)} %get-tuple-element.61), custom_call_target="InvertDiagBlocksLowerTriangular" | custom-call | tf_op jit(solution)/shard_map/jit(cholesky)/cholesky | solution.py:183
  275.7 11.7 %cholesky.540 = f32[128,128]{1,0:T(8,128)S(1)} custom-call(f32[128,128]{1,0:T(8,128)S(1)} %cholesky.641), custom_call_target="Cholesky" | custom-call | tf_op jit(solution)/shard_map/jit(cholesky)/cholesky | solution.py:183
  288.7 10.2 %custom-call.90 = f32[1,128,128]{1,2,0:T(8,128)S(1)} custom-call(f32[1,128,128]{2,1,0:T(8,128)S(1)} %get-tuple-element.58), custom_call_target="InvertDiagBlocksLowerTriangular" | custom-call | tf_op jit(solution)/shard_map/jit(cholesky)/cholesky | solution.py:183
  302.2 11.7 %cholesky.560 = f32[128,128]{1,0:T(8,128)S(1)} custom-call(f32[128,128]{1,0:T(8,128)S(1)} %cholesky.646), custom_call_target="Cholesky" | custom-call | tf_op jit(solution)/shard_map/jit(cholesky)/cholesky | solution.py:183
  315.3 9.8 %custom-call.91 = f32[1,128,128]{1,2,0:T(8,128)S(1)} custom-call(f32[1,128,128]{2,1,0:T(8,128)S(1)} %get-tuple-element.55), custom_call_target="InvertDiagBlocksLowerTriangular" | custom-call | tf_op jit(solution)/shard_map/jit(cholesky)/cholesky | solution.py:183
  328.1 11.9 %cholesky.580 = f32[128,128]{1,0:T(8,128)S(1)} custom-call(f32[128,128]{1,0:T(8,128)S(1)} %cholesky.651), custom_call_target="Cholesky" | custom-call | tf_op jit(solution)/shard_map/jit(cholesky)/cholesky | solution.py:183
  341.3 9.8 %custom-call.92 = f32[1,128,128]{1,2,0:T(8,128)S(1)} custom-call(f32[1,128,128]{2,1,0:T(8,128)S(1)} %get-tuple-element.52), custom_call_target="InvertDiagBlocksLowerTriangular" | custom-call | tf_op jit(solution)/shard_map/jit(cholesky)/cholesky | solution.py:183
  353.7 11.7 %cholesky.598 = f32[128,128]{1,0:T(8,128)S(1)} custom-call(f32[128,128]{1,0:T(8,128)S(1)} %convolution_subtract_fusion.21), custom_call_target="Cholesky" | custom-call | tf_op jit(solution)/shard_map/jit(cholesky)/cholesky | solution.py:183
  372.4 4.9 select_select_fusion
  377.3 28.1 %while.1 = (s32[]{:T(128)}, f32[1024,1024]{1,0:T(8,128)}, s32[8,2]{0,1:T(2,128)S(1)}, f32[8,128,128]{2,1,0:T(8,128)}, s32[]{:T(128)}) while((s32[]{:T(128)}, f32[1024,1024]{1,0:T(8,128)}, s32[8,2]{0,1:T(2,128)S(1)}, f32[8,128,128]{2,1,0:T(8,128)}, s32[]{:T(128)}) %tuple.84), condition=%wide.while_cond, body=%wide.while_body.sunk | while | flops 2 | bytes 132705 | solution.py:21
  405.4 79.6 %custom-call.93 = f32[8,128,128]{1,2,0:T(8,128)S(1)} custom-call(f32[8,128,128]{2,1,0:T(8,128)} %get-tuple-element.13), custom_call_target="InvertDiagBlocksLowerTriangular" | custom-call | tf_op jit(solution)/shard_map/jit(_solve_triangular)/triangular_solve | solution.py:21
  511.5 11.7 %custom-call.94 = f32[2,64,64]{2,1,0:T(8,128)S(1)} custom-call(f32[2,64,64]{2,1,0:T(8,128)S(1)} %fusion.264), custom_call_target="Cholesky" | custom-call | tf_op jit(solution)/shard_map/vmap(jit(cholesky))/cholesky | solution.py:61
  523.5 10.2 %custom-call.95 = f32[2,1,64,64]{2,3,1,0:T(8,128)S(1)} custom-call(f32[2,1,64,64]{3,2,1,0:T(8,128)S(1)} %select_bitcast_fusion), custom_call_target="InvertDiagBlocksLowerTriangular" | custom-call | tf_op jit(solution)/shard_map/vmap(jit(_solve_triangular))/triangular_solve | solution.py:62
  557.1 9.7 %slice.592 = f32[3,1024,1024]{2,0,1:T(4,128)S(1)} slice(f32[4,1024,1024]{2,0,1:T(4,128)} %all-gather.5.cloned.1.call-done), slice={[1:4], [0:1024], [0:1024]} | slice | bytes 25165824 | tf_op jit(solution)/shard_map/slice | solution.py:191
  566.8 20.2 %fusion.23 = f32[3,64,1024]{2,1,0:T(8,128)S(1)} fusion(f32[3,1024,1024]{2,0,1:T(4,128)S(1)} %slice.592, f32[1024,64]{0,1:T(8,128)S(1)} %constant_dynamic-update-slice_fusion.36), kind=kOutput, calls=%fused_computation.33 | convolution fusion | flops 2415919104 | bytes 13631488 | tf_op jit(solution)/shard_map/aj,tij->tai/dot_general | solution.py:191
  608.1 4.4 copy.180
  618.5 5.3 copy.182
  623.8 5.3 fusion.3
  (324 shorter events, 210.6 us)
Async XLA Ops:
  6.5 56.1 %all-gather.3.cloned.1.call-start = ((), (), s32[]{:S(2)}) async-start(), calls=%async_computation.1 | async-start | bytes 2162688 | tf_op jit(solution)/shard_map/all_gather | solution.py:186
  8.0 134.1 %all-gather.5.cloned.1.call-start = ((), (), s32[]{:S(2)}) async-start(), calls=%async_computation.2 | async-start | bytes 17301504 | tf_op jit(solution)/shard_map/all_gather | solution.py:181
  13.9 11.1 %copy-start.28 = (s32[2,1]{0,1:T(1,128)S(1)}, s32[2,1]{0,1:T(1,128)}, u32[]{:S(2)}) copy-start(s32[2,1]{0,1:T(1,128)} %param.19) | copy-start | bytes 28
  13.9 11.2 %copy-start.29 = (s32[2]{0:T(128)S(1)}, s32[2]{0:T(128)}, u32[]{:S(2)}) copy-start(s32[2]{0:T(128)} %param.16) | copy-start | bytes 28
  13.9 11.3 %copy-start.30 = (s32[2,1]{0,1:T(1,128)S(1)}, s32[2,1]{0,1:T(1,128)}, u32[]{:S(2)}) copy-start(s32[2,1]{0,1:T(1,128)} %param.18) | copy-start | bytes 28
  13.9 106.0 %all-to-all-start = ((f32[8,2,8,64,128]{4,3,1,2,0:T(8,128)}), f32[8,2,8,64,128]{4,3,1,2,0:T(8,128)}, u32[]{:S(2)}, u32[]{:S(2)}) async-start(f32[8,2,8,64,128]{4,3,1,2,0:T(8,128)} %stack.10), calls=%async_computation | async-start | bytes 8388608 | tf_op jit(solution)/shard_map/all_to_all | solution.py:175
  25.3 3.2 copy-start.12
  28.5 5.9 copy-start.1
  29.2 3.1 copy-start.13
  66.8 442.1 %copy-start.15 = (f32[2,64,64]{2,1,0:T(8,128)}, f32[2,64,64]{2,1,0:T(8,128)S(1)}, u32[]{:S(2)}) copy-start(f32[2,64,64]{2,1,0:T(8,128)S(1)} %fusion.38) | copy-start | bytes 98308
  123.1 2.0 copy-start.2
  500.6 10.9 %copy-start.27 = (pred[64,64]{1,0:T(8,128)(4,1)S(1)}, pred[64,64]{1,0:T(8,128)(4,1)}, u32[]{:S(2)}) copy-start(pred[64,64]{1,0:T(8,128)(4,1)} %get-tuple-element.120) | copy-start | bytes 12292
  501.9 21.6 %copy-start.25 = (pred[64,64]{1,0:T(8,128)(4,1)S(1)}, pred[64,64]{1,0:T(8,128)(4,1)}, u32[]{:S(2)}) copy-start(pred[64,64]{1,0:T(8,128)(4,1)} %iota_compare_fusion.5) | copy-start | bytes 12292
  509.1 14.3 %copy-start.18 = (f32[2,64,64]{2,1,0:T(8,128)}, f32[2,64,64]{2,1,0:T(8,128)S(1)}, u32[]{:S(2)}) copy-start(f32[2,64,64]{2,1,0:T(8,128)S(1)} %fusion.331) | copy-start | bytes 98308
  523.3 23.7 %copy-start.20 = (f32[2,64,64]{2,1,0:T(8,128)}, f32[2,64,64]{2,1,0:T(8,128)S(1)}, u32[]{:S(2)}) copy-start(f32[2,64,64]{2,1,0:T(8,128)S(1)} %custom-call.94) | copy-start | bytes 98308
  533.8 11.8 %copy-start = (f32[1024,1024]{1,0:T(8,128)S(1)}, f32[1024,1024]{1,0:T(8,128)}, u32[]{:S(2)}) copy-start(f32[1024,1024]{1,0:T(8,128)} %get-tuple-element.168) | copy-start | bytes 12582916
  566.8 20.2 %copy-start.24 = (f32[2,64,64]{2,1,0:T(8,128)S(1)}, f32[2,64,64]{2,1,0:T(8,128)}, u32[]{:S(2)}) copy-start(f32[2,64,64]{2,1,0:T(8,128)} %fusion.54) | copy-start | bytes 98308
  566.8 21.8 %copy-start.23 = (f32[2,64,64]{2,1,0:T(8,128)S(1)}, f32[2,64,64]{2,1,0:T(8,128)}, u32[]{:S(2)}) copy-start(f32[2,64,64]{2,1,0:T(8,128)} %fusion.53) | copy-start | bytes 98308
  566.8 24.6 %copy-start.22 = (f32[2,64,64]{2,1,0:T(8,128)S(1)}, f32[2,64,64]{2,1,0:T(8,128)}, u32[]{:S(2)}) copy-start(f32[2,64,64]{2,1,0:T(8,128)} %fusion.52) | copy-start | bytes 98308
  587.0 6.5 copy-start.16
  588.5 8.1 %copy-start.11 = (f32[2,3,64,1024]{3,2,0,1:T(8,128)S(1)}, f32[2,3,64,1024]{3,2,0,1:T(8,128)}, u32[]{:S(2)}) copy-start(f32[2,3,64,1024]{3,2,0,1:T(8,128)} %get-tuple-element.28) | copy-start | bytes 4718596
  588.6 8.1 %copy-start.19 = (f32[2,64,64]{2,1,0:T(8,128)S(1)}, f32[2,64,64]{2,1,0:T(8,128)}, u32[]{:S(2)}) copy-start(f32[2,64,64]{2,1,0:T(8,128)} %copy-done.18) | copy-start | bytes 98308
  594.1 7.0 %copy-start.7 = (f32[2,3,64,1024]{3,2,0,1:T(8,128)S(1)}, f32[2,3,64,1024]{3,2,0,1:T(8,128)}, u32[]{:S(2)}) copy-start(f32[2,3,64,1024]{3,2,0,1:T(8,128)} %get-tuple-element.27) | copy-start | bytes 4718596
  594.1 7.0 %copy-start.9 = (f32[2,64,3,1024]{3,1,2,0:T(8,128)S(1)}, f32[2,64,3,1024]{3,1,2,0:T(8,128)}, u32[]{:S(2)}) copy-start(f32[2,64,3,1024]{3,1,2,0:T(8,128)} %fusion.64) | copy-start | bytes 4718596
  594.1 7.0 %copy-start.14 = (f32[2,64,64]{2,1,0:T(8,128)S(1)}, f32[2,64,64]{2,1,0:T(8,128)}, u32[]{:S(2)}) copy-start(f32[2,64,64]{2,1,0:T(8,128)} %copy-done.13) | copy-start | bytes 98308
  604.4 11.2 %copy-start.21 = (f32[2,64,64]{2,1,0:T(8,128)S(1)}, f32[2,64,64]{2,1,0:T(8,128)}, u32[]{:S(2)}) copy-start(f32[2,64,64]{2,1,0:T(8,128)} %copy-done.20) | copy-start | bytes 98308
  604.4 11.2 %copy-start.26 = (pred[64,64]{1,0:T(8,128)(4,1)S(1)}, pred[64,64]{1,0:T(8,128)(4,1)}, u32[]{:S(2)}) copy-start(pred[64,64]{1,0:T(8,128)(4,1)} %iota_compare_fusion.5) | copy-start | bytes 12292
  639.2 4.5 copy-start.17
  639.2 4.7 copy-start.4
  643.9 6.1 copy-start.10
  650.0 5.3 copy-start.8
  652.2 7.6 %copy-start.6 = (f32[2,3,64,1024]{3,2,0,1:T(8,128)S(1)}, f32[2,3,64,1024]{3,2,0,1:T(8,128)}, u32[]{:S(2)}) copy-start(f32[2,3,64,1024]{3,2,0,1:T(8,128)} %get-tuple-element.24) | copy-start | bytes 4718596
  (2 other events, 3.3 us)
Sparse Core Ops, SparseCore 0:
  9.9 52.6 all-gather.2
  65.2 76.9 all-gather.4
